TPU v7x, 32 devices: a whole 2x2x4 slice. The times are simulated.
32 devices in a mesh: row: 8 (over y, x, core), col: 4 (over z).
Axes of the slice: x: 2, y: 2, z: 4, core: 2. Of those that a mesh axis runs over, the one named last changes fastest.
Arguments:
- inputs: bfloat16 [32768, 261], P('row'), may hold values from -6 to 6
- latent: bfloat16 [512, 1024], P('row', 'col'), may hold values from -6 to 6
- gain_latent: float32 [1024], P('col'), may hold values from 0.25 to 1.75
- gain_inputs: float32 [261], replicated, may hold values from 0.25 to 1.75
- cross_query: bfloat16 [1024, 1024], P('col', 'row'), may hold values from -0.1875 to 0.1875
- cross_keys: bfloat16 [261, 1024], P(None, 'col'), may hold values from -0.375 to 0.375
- cross_values: bfloat16 [261, 1024], P(None, 'col'), may hold values from -0.375 to 0.375
- cross_output: bfloat16 [1024, 1024], P('col', 'row'), may hold values from -3 to 3
- cross_gain: float32 [1024], P('col'), may hold values from 0.25 to 1.75
- cross_up: bfloat16 [1024, 1024], P('row', 'col'), may hold values from -0.1875 to 0.1875
- cross_down: bfloat16 [1024, 1024], P('col', 'row'), may hold values from -0.1875 to 0.1875
- self_gain: float32 [1024], P('col'), may hold values from 0.25 to 1.75
- self_query: bfloat16 [1024, 1024], P('row', 'col'), may hold values from -0.1875 to 0.1875
- self_keys: bfloat16 [1024, 1024], P('row', 'col'), may hold values from -0.1875 to 0.1875
- self_values: bfloat16 [1024, 1024], P('row', 'col'), may hold values from -0.1875 to 0.1875
- self_output: bfloat16 [1024, 1024], P('col', 'row'), may hold values from -2 to 2
- self_mlp_gain: float32 [1024], P('col'), may hold values from 0.25 to 1.75
- self_mlp_up: bfloat16 [1024, 1024], P('row', 'col'), may hold values from -0.1875 to 0.1875
- self_mlp_down: bfloat16 [1024, 1024], P('col', 'row'), may hold values from -0.1875 to 0.1875
- cotangent: bfloat16 [16384, 1024], P('row', 'col'), may hold values from -6 to 6
Outputs:
- result: bfloat16 [16384, 1024], P('row', 'col')
- grad_inputs: float32 [32768, 261], P(('row', 'col'))
- grad_latent: float32 [512, 1024], P('row', 'col')
- grad_gain_latent: float32 [1024], P('col')
- grad_gain_inputs: float32 [261], replicated
- grad_cross_query: float32 [1024, 1024], P('col', 'row')
- grad_cross_keys: float32 [261, 1024], P(None, 'col')
- grad_cross_values: float32 [261, 1024], P(None, 'col')
- grad_cross_output: float32 [1024, 1024], P('col', 'row')
- grad_cross_gain: float32 [1024], P('col')
- grad_cross_up: float32 [1024, 1024], P('row', 'col')
- grad_cross_down: float32 [1024, 1024], P('col', 'row')
- grad_self_gain: float32 [1024], P('col')
- grad_self_query: float32 [1024, 1024], P('row', 'col')
- grad_self_keys: float32 [1024, 1024], P('row', 'col')
- grad_self_values: float32 [1024, 1024], P('row', 'col')
- grad_self_output: float32 [1024, 1024], P('col', 'row')
- grad_self_mlp_gain: float32 [1024], P('col')
- grad_self_mlp_up: float32 [1024, 1024], P('row', 'col')
- grad_self_mlp_down: float32 [1024, 1024], P('col', 'row')
All inputs are finite; a program needn't handle non-finite values.
Results may differ from a plain program's by a relative error of at most 0.039.
Values may be sent and summed in bfloat16 or wider, within the bound.
No kernel may reach another device: no remote copies, remote signals or barrier semaphores. Data moves between devices by JAX's collectives and lax.ppermute only.
A program may use at most 192 MiB of HBM per device.

v0:
```python
import jax
import jax.numpy as jnp
from jax import lax
from jax.sharding import PartitionSpec as P

HEADS = 8
M = 1024
EPSILON = 1e-05
BF = jnp.bfloat16
F32 = jnp.float32
BOTH = ("row", "col")


def nn(left, right):
    return lax.dot_general(left, right, (((1,), (0,)), ((), ())), preferred_element_type=F32)


def nt(left, right):
    return lax.dot_general(left, right, (((1,), (1,)), ((), ())), preferred_element_type=F32)


def tn(left, right):
    return lax.dot_general(left, right, (((0,), (0,)), ((), ())), preferred_element_type=F32)


def norm(values, gain):
    average = jnp.mean(values, axis=-1, keepdims=True)
    centred = values - average
    scale = lax.rsqrt(jnp.mean(centred * centred, axis=-1, keepdims=True) + EPSILON)
    hat = centred * scale
    return ((hat * gain).astype(BF), hat, scale)


def norm_back(upstream, gain, hat, scale):
    scaled = upstream * gain
    first = jnp.mean(scaled, axis=-1, keepdims=True)
    second = jnp.mean(scaled * hat, axis=-1, keepdims=True)
    return (scale * (scaled - first - hat * second), jnp.sum(upstream * hat, axis=0))


def gelu(values):
    return jax.nn.gelu(values, approximate=True)


def gelu_back(values, upstream):
    return jax.vjp(gelu, values)[1](upstream)[0].astype(BF)


def softmax(scores):
    exponent = jnp.exp(scores - jnp.max(scores, axis=-1, keepdims=True))
    return exponent / jnp.sum(exponent, axis=-1, keepdims=True)


def softmax_back(soft, upstream):
    return (soft * (upstream - jnp.sum(upstream * soft, axis=-1, keepdims=True))).astype(BF)


def local(
    inputs,
    latent,
    gain_latent,
    gain_inputs,
    cross_query,
    cross_keys,
    cross_values,
    cross_output,
    cross_gain,
    cross_up,
    cross_down,
    self_gain,
    self_query,
    self_keys,
    self_values,
    self_output,
    self_mlp_gain,
    self_mlp_up,
    self_mlp_down,
    cotangent,
):
    cols = lax.axis_size("col")
    rows = lax.axis_size("row")
    place = lax.axis_index("col")
    wide = latent.shape[1] * cols
    block = latent.shape[1]
    lat_count = latent.shape[0] * rows
    head_size = wide // HEADS
    in_width = inputs.shape[1]
    images = inputs.shape[0] // M
    share = max(1, cols // images)
    assert images * share == cols
    here = lat_count // share
    groups = [[image * share + part for part in range(share)] for image in range(images)]
    cross_scale = wide ** (-0.5)
    self_scale = head_size ** (-0.5)
    by_row = (cross_up, self_query, self_keys, self_values, self_mlp_up)
    by_col = (cross_query, cross_output, cross_down, self_output, self_mlp_down)
    stack = jnp.stack([item.T for item in by_col] + list(by_row))
    count = stack.shape[0]
    deep = stack.shape[1]
    whole = lax.all_gather(stack, BOTH, axis=0, tiled=False)
    whole = whole.reshape(rows, cols, count, deep, block)
    whole = whole.transpose(2, 0, 3, 1, 4).reshape(count, wide, wide)
    t_query, t_output, t_down, t_self_output, t_self_down, up, s_query, s_keys, s_values, s_up = [
        whole[index] for index in range(count)
    ]
    lat_all = lax.all_gather(latent, BOTH, axis=0, tiled=False)
    lat_all = lat_all.reshape(rows, cols, -1, block).transpose(0, 2, 1, 3).reshape(lat_count, wide)
    pair = lax.all_gather(jnp.concatenate([cross_keys, cross_values]), "col", axis=1, tiled=True)
    c_keys, c_values = (pair[:in_width], pair[in_width:])
    gains = lax.all_gather(
        jnp.stack([gain_latent, cross_gain, self_gain, self_mlp_gain]), "col", axis=1, tiled=True
    )
    g_lat, g_cross, g_self, g_mlp = [gains[index] for index in range(4)]
    grad_out_low = lax.all_to_all(cotangent, "col", split_axis=0, concat_axis=1, tiled=True)
    start = place % share * here
    lat = lax.dynamic_slice_in_dim(lat_all, start, here, axis=0).astype(F32)
    pixels = lax.dynamic_slice_in_dim(inputs, place // share * M, M, axis=0).astype(F32)
    lat_low, lat_hat, lat_scale = norm(lat, g_lat)
    queries = nt(lat_low, t_query).astype(BF)
    pix_low, pix_hat, pix_scale = norm(pixels, gain_inputs)
    key_rows = nn(pix_low, c_keys).astype(BF)
    values = nn(pix_low, c_values).astype(BF)
    soft = softmax(nt(queries, key_rows) * cross_scale)
    soft_low = soft.astype(BF)
    attended = nn(soft_low, values).astype(BF)
    state_one = lat + nt(attended, t_output)
    mlp_low, mlp_hat, mlp_scale = norm(state_one, g_cross)
    hidden = nn(mlp_low, up)
    active = gelu(hidden).astype(BF)
    state_two = state_one + nt(active, t_down)
    attn_low, attn_hat, attn_scale = norm(state_two, g_self)
    head_q = nn(attn_low, s_query).astype(BF)
    head_k = nn(attn_low, s_keys).astype(BF)
    head_v = nn(attn_low, s_values).astype(BF)
    if share > 1:
        head_k, head_v = [
            lax.all_gather(item, "col", axis_index_groups=groups, axis=0, tiled=True)
            for item in (head_k, head_v)
        ]

    def split(item):
        return item.reshape(item.shape[0], HEADS, head_size)

    def join(item):
        return item.astype(BF).reshape(item.shape[0], wide)

    def contract(form, left, right):
        return jnp.einsum(form, left, right, preferred_element_type=F32)

    hq, hk, hv = (split(head_q), split(head_k), split(head_v))
    self_soft = softmax(contract("qhd,khd->hqk", hq, hk) * self_scale)
    self_soft_low = self_soft.astype(BF)
    self_att = join(contract("hqk,khd->qhd", self_soft_low, hv))
    state_three = state_two + nt(self_att, t_self_output)
    last_low, last_hat, last_scale = norm(state_three, g_mlp)
    hidden_two = nn(last_low, s_up)
    active_two = gelu(hidden_two).astype(BF)
    result = (state_three + nt(active_two, t_self_down)).astype(BF)
    result = lax.all_to_all(result, "col", split_axis=1, concat_axis=0, tiled=True)
    grad_self_down = tn(grad_out_low, active_two)
    dh2 = gelu_back(hidden_two, nn(grad_out_low, t_self_down))
    grad_self_up = tn(last_low, dh2)
    back, gain_mlp = norm_back(nt(dh2, s_up), g_mlp, last_hat, last_scale)
    g3 = grad_out_low.astype(F32) + back
    g3_low = g3.astype(BF)
    grad_self_output = tn(g3_low, self_att)
    d_att = split(nn(g3_low, t_self_output).astype(BF))
    d_self = softmax_back(self_soft, contract("qhd,khd->hqk", d_att, hv))
    dq = join(contract("hqk,khd->qhd", d_self, hk) * self_scale)
    dk = contract("hqk,qhd->khd", d_self, hq) * self_scale
    dvv = contract("hqk,qhd->khd", self_soft_low, d_att)
    dk, dvv = (join(dk), join(dvv))
    if share > 1:
        dk, dvv = [
            lax.psum_scatter(item, "col", axis_index_groups=groups, scatter_dimension=0, tiled=True)
            for item in (dk, dvv)
        ]
    grad_query, grad_keys, grad_values = (tn(attn_low, dq), tn(attn_low, dk), tn(attn_low, dvv))
    dy = nt(dq, s_query) + nt(dk, s_keys) + nt(dvv, s_values)
    back, gain_self = norm_back(dy, g_self, attn_hat, attn_scale)
    g2 = g3 + back
    g2_low = g2.astype(BF)
    grad_down = tn(g2_low, active)
    dh1 = gelu_back(hidden, nn(g2_low, t_down))
    grad_up = tn(mlp_low, dh1)
    back, gain_cross = norm_back(nt(dh1, up), g_cross, mlp_hat, mlp_scale)
    g1 = g2 + back
    g1_low = g1.astype(BF)
    grad_output = tn(g1_low, attended)
    d_attended = nn(g1_low, t_output).astype(BF)
    d_scores = softmax_back(soft, nt(d_attended, values))
    d_queries = (nn(d_scores, key_rows) * cross_scale).astype(BF)
    d_keys = (tn(d_scores, queries) * cross_scale).astype(BF)
    d_values = tn(soft_low, d_attended).astype(BF)
    grad_cross_query = tn(d_queries, lat_low)
    grad_pair = jnp.concatenate([tn(pix_low, d_keys), tn(pix_low, d_values)])
    d_pix = nt(d_keys, c_keys) + nt(d_values, c_values)
    grad_inputs, gain_pix = norm_back(d_pix, gain_inputs, pix_hat, pix_scale)
    if share > 1:
        grad_inputs = lax.psum_scatter(
            grad_inputs, "col", axis_index_groups=groups, scatter_dimension=0, tiled=True
        )
    back, gain_lat = norm_back(nn(d_queries, t_query), g_lat, lat_hat, lat_scale)
    grad_lat = g1 + back
    if share > 1:
        grad_lat = lax.dynamic_update_slice_in_dim(
            jnp.zeros((lat_count, wide), F32), grad_lat, start, axis=0
        )

    def reduce(item):
        item = lax.psum_scatter(item, "row", scatter_dimension=0, tiled=False)
        return lax.psum_scatter(item, "col", scatter_dimension=0, tiled=False).astype(F32)

    grads = jnp.stack(
        [
            item.astype(BF)
            for item in (
                grad_cross_query,
                grad_output,
                grad_down,
                grad_self_output,
                grad_self_down,
                grad_up,
                grad_query,
                grad_keys,
                grad_values,
                grad_self_up,
            )
        ]
    )
    grads = grads.reshape(count, rows, deep, cols, block).transpose(1, 3, 0, 2, 4)
    grads = reduce(grads)
    grad_lat = reduce(grad_lat.astype(BF).reshape(rows, -1, cols, block).transpose(0, 2, 1, 3))
    grad_pair = lax.psum_scatter(
        grad_pair.astype(BF).reshape(-1, cols, block).transpose(1, 0, 2),
        "col",
        scatter_dimension=0,
        tiled=False,
    )
    grad_pair = lax.psum(grad_pair, "row").astype(F32)
    gain_all, gain_pix = lax.psum(
        (jnp.stack([gain_lat, gain_cross, gain_self, gain_mlp]), gain_pix), BOTH
    )
    gain_all = lax.dynamic_slice_in_dim(gain_all, place * block, block, axis=1)
    return (
        result,
        grad_inputs,
        grad_lat,
        gain_all[0],
        gain_pix,
        grads[0].T,
        grad_pair[:in_width],
        grad_pair[in_width:],
        grads[1].T,
        gain_all[1],
        grads[5],
        grads[2].T,
        gain_all[2],
        grads[6],
        grads[7],
        grads[8],
        grads[3].T,
        gain_all[3],
        grads[9],
        grads[4].T,
    )


def solution(mesh):
    rc, cr, c, cc = (P("row", "col"), P("col", "row"), P("col"), P(None, "col"))
    return jax.shard_map(
        local,
        mesh=mesh,
        in_specs=(
            P("row", None),
            rc,
            c,
            P(),
            cr,
            cc,
            cc,
            cr,
            c,
            rc,
            cr,
            c,
            rc,
            rc,
            rc,
            cr,
            c,
            rc,
            cr,
            rc,
        ),
        out_specs=(
            rc,
            P(BOTH, None),
            rc,
            c,
            P(),
            cr,
            cc,
            cc,
            cr,
            c,
            rc,
            cr,
            c,
            rc,
            rc,
            rc,
            cr,
            c,
            rc,
            cr,
        ),
        check_vma=False,
    )
```

profile of v0, /device:TPU:0, one launch (start us, length us, event | category | flops | bytes accessed | tf_op | source)
XLA Modules:
  0.0 815.1 jit_solution(8326261063209987246)
XLA Ops:
  15.9 6.4 all-to-all-start.1
  22.3 46.8 %all_gather.20 = f32[4,1024]{1,0:T(4,128)S(1)} all-gather(f32[4,256]{1,0:T(4,128)S(1)} %pad_maximum_fusion.2), channel_id=1, replica_groups=mesh['row'=8,'col'=4] {'col'}, dimensions={1}, use_global_device_ids=true | all-gather | bytes 20480 | tf_op jit(solution)/shard_map/all_gather | solution.py:110
  69.7 4.1 convolution_convert_fusion.10
  73.9 4.5 fusion.166
  78.3 41.6 %all-gather.8.cloned.1.call-done = bf16[2048,256]{1,0:T(8,128)(2,1)} async-done(((bf16[64,256]{1,0:T(8,128)(2,1)}), bf16[2048,256]{1,0:T(8,128)(2,1)}) %all-gather.8.cloned.1.call-update) | async-done | bytes 1048592 | tf_op jit(solution)/shard_map/all_gather | solution.py:106
  119.9 2.0 copy.114
  126.0 7.4 multiply_reduce_fusion.14
  135.5 120.6 %all-gather.10.cloned.1.call-done = bf16[320,128,256]{2,1,0:T(8,128)(2,1)} async-done(((bf16[10,128,256]{2,1,0:T(8,128)(2,1)}), bf16[320,128,256]{2,1,0:T(8,128)(2,1)}) %all-gather.10.cloned.1.call-update) | async-done | bytes 20971536 | tf_op jit(solution)/shard_map/all_gather | solution.py:100
  256.1 30.8 %copy.120 = bf16[8,4,10,128,256]{3,0,4,1,2:T(8,128)(2,1)} copy(bf16[8,4,10,128,256]{4,3,2,1,0:T(8,128)(2,1)} %bitcast.339) | data formatting | bytes 41943040 | tf_op jit(solution)/shard_map/reshape | solution.py:101
  286.9 14.1 %fusion.177 = (bf16[1,8,128,4,256]{2,1,4,3,0:T(8,128)(2,1)}, bf16[1,8,128,4,256]{2,1,4,3,0:T(8,128)(2,1)}, bf16[1,8,128,4,256]{2,1,4,3,0:T(8,128)(2,1)}, bf16[1,...) fusion(bf16[10,8,128,4,256]{2,1,4,3,0:T(8,128)(2,1)} %bitcast.338), kind=kLoop, calls=%fused_computation.268 | loop fusion | bytes 41943040 | tf_op jit(solution)/shard_map/slice | solution.py:104
  303.3 2.6 fusion.185
  305.9 5.8 online-softmax
  311.8 4.2 fusion.181
  323.1 2.3 fusion.131
  325.4 2.3 fusion.114
  327.7 2.3 copy.159
  329.9 4.2 fusion.117
  334.1 2.5 copy.160
  336.6 7.6 fusion.183
  344.1 4.7 fusion.99
  354.4 2.4 fusion.18
  360.6 2.3 fusion.120
  362.9 2.6 copy.161
  365.6 5.3 fusion.102
  370.9 4.4 multiply_reduce_fusion
  375.6 2.5 multiply_convert_fusion
  390.4 2.8 fusion.11
  400.1 2.8 convolution_convert_fusion.9
  404.1 2.7 multiply_convert_fusion.1
  410.7 2.8 convolution_convert_fusion.8
  413.5 2.9 convolution_convert_fusion.7
  416.5 2.8 convolution_convert_fusion.6
  419.2 2.6 convolution_convert_fusion.5
  421.9 2.9 convert_bitcast_fusion
  424.8 2.8 convolution_convert_fusion.4
  427.5 2.7 convolution_convert_fusion.3
  430.2 2.7 convolution_convert_fusion.2
  432.8 2.6 convolution_convert_fusion.1
  435.5 2.8 convolution_convert_fusion
  441.5 4.6 stack.117
  446.1 2.8 stack.118
  448.9 4.7 stack.119
  453.6 2.7 stack.120
  456.4 2.2 copy.177
  458.6 2.6 copy.141
  461.1 4.6 stack.122
  465.8 2.8 stack.123
  468.6 4.7 stack.124
  473.3 2.8 stack.125
  476.1 3.4 stack.126
  479.5 2.6 convolution_convert_fusion.11
  482.5 3.4 convolution_convert_fusion.12
  488.8 3.5 copy_dynamic-update-slice_fusion.8
  496.2 3.5 copy_dynamic-update-slice_fusion.5
  513.0 9.4 %reduce-scatter.14.cloned.1.call-done = bf16[1,522,256]{2,1,0:T(8,128)(2,1)} async-done(((bf16[4,522,256]{2,1,0:T(8,128)(2,1)}), bf16[1,522,256]{2,1,0:T(8,128)(2,1)}) %reduce-scatter.14.cloned.1.call-update) | async-done | bytes 267280 | tf_op jit(solution)/shard_map/reduce_scatter | solution.py:234
  522.5 138.4 %reduce-scatter.10.cloned.1.call-done = bf16[1,4,10,128,256]{4,3,2,1,0:T(8,128)(2,1)} async-done(((bf16[8,4,10,128,256]{4,3,2,1,0:T(8,128)(2,1)}), bf16[1,4,10,128,256]{4,3,2,1,0:T(8,128)(2,1)}) %reduce-scatter.10.cloned.1.call-update) | async-done | bytes 2621456 | tf_op jit(solution)/shard_map/reduce_scatter | solution.py:211
  660.9 3.8 add_convert_fusion.1
  665.7 4.8 all-to-all-start
  670.5 2.6 fusion.168
  673.8 2.0 fusion.144
  675.9 41.5 %all-reduce = (f32[4,1024]{1,0:T(4,128)S(1)}, f32[261]{0:T(512)}) all-reduce(f32[4,1024]{1,0:T(4,128)S(1)} %pad_maximum_fusion.1, f32[261]{0:T(512)S(1)} %get-tuple-element.68), channel_id=1, replica_groups=mesh['row'=8,'col'=4] {'row','col'}, use_global_device_ids=true, to_apply=%region_32.33 | all-reduce | flops 4357 | bytes 34856 | tf_op jit(solution)/shard_map/psum | solution.py:241
  718.0 2.5 fusion.143
  721.9 24.2 %all-reduce.3.cloned.1.call-done = bf16[522,256]{1,0:T(8,128)(2,1)} async-done(((bf16[522,256]{1,0:T(8,128)(2,1)}), bf16[522,256]{1,0:T(8,128)(2,1)}) %all-reduce.3.cloned.1.call-update) | async-done | bytes 267280 | tf_op jit(solution)/shard_map/psum | solution.py:240
  748.0 53.6 %reduce-scatter.12.cloned.1.call-done = bf16[1,10,128,256]{3,2,1,0:T(8,128)(2,1)} async-done(((bf16[4,10,128,256]{3,2,1,0:T(8,128)(2,1)}), bf16[1,10,128,256]{3,2,1,0:T(8,128)(2,1)}) %reduce-scatter.12.cloned.1.call-update) | async-done | bytes 655376 | tf_op jit(solution)/shard_map/reduce_scatter | solution.py:212
  (286 shorter events, 94.2 us)
Async XLA Ops:
  7.2 7.7 copy-start.47
  7.2 7.7 copy-start.48
  7.2 7.8 copy-start.49
  7.2 7.8 copy-start.50
  7.2 7.8 copy-start.51
  7.2 62.5 %all-gather.6.cloned.1.call-start = ((), (), s32[]{:S(2)}) async-start(), calls=%async_computation.7 | async-start | bytes 1351680 | tf_op jit(solution)/shard_map/all_gather | solution.py:108
  9.1 110.8 %all-gather.8.cloned.1.call-start = ((), (), s32[]{:S(2)}) async-start(), calls=%async_computation.14 | async-start | bytes 1081344 | tf_op jit(solution)/shard_map/all_gather | solution.py:106
  9.8 246.3 %all-gather.10.cloned.1.call-start = ((), (), s32[]{:S(2)}) async-start(), calls=%async_computation.15 | async-start | bytes 21626880 | tf_op jit(solution)/shard_map/all_gather | solution.py:100
  12.7 9.5 %copy-start.58 = (f32[256]{0:T(256)S(1)}, f32[256]{0:T(256)}, u32[]{:S(2)}) copy-start(f32[256]{0:T(256)} %param.36) | copy-start | bytes 3076
  12.7 9.5 %copy-start.59 = (f32[256]{0:T(256)S(1)}, f32[256]{0:T(256)}, u32[]{:S(2)}) copy-start(f32[256]{0:T(256)} %param.31) | copy-start | bytes 3076
  12.8 9.5 %copy-start.60 = (f32[256]{0:T(256)S(1)}, f32[256]{0:T(256)}, u32[]{:S(2)}) copy-start(f32[256]{0:T(256)} %param.28) | copy-start | bytes 3076
  12.8 9.5 %copy-start.61 = (f32[256]{0:T(256)S(1)}, f32[256]{0:T(256)}, u32[]{:S(2)}) copy-start(f32[256]{0:T(256)} %param.22) | copy-start | bytes 3076
  13.7 55.4 %copy-start.41 = (bf16[4096,261]{0,1:T(8,128)(2,1)S(1)}, bf16[4096,261]{0,1:T(8,128)(2,1)}, u32[]{:S(2)}) copy-start(bf16[4096,261]{0,1:T(8,128)(2,1)} %param.20) | copy-start | bytes 6414340
  15.9 53.6 %all-to-all-start.1 = ((bf16[4,512,256]{2,1,0:T(8,128)(2,1)}), bf16[4,512,256]{2,1,0:T(8,128)(2,1)S(1)}, u32[]{:S(2)}, u32[]{:S(2)}) async-start(bf16[4,512,256]{2,1,0:T(8,128)(2,1)} %bitcast.381), calls=%async_computation.1 | async-start | bytes 2097152 | tf_op jit(solution)/shard_map/all_to_all | solution.py:114
  22.3 47.4 %copy-start.56 = (f32[261]{0:T(512)S(1)}, f32[261]{0:T(512)}, u32[]{:S(2)}) copy-start(f32[261]{0:T(512)} %param.23) | copy-start | bytes 3136
  22.3 490.0 %reduce-scatter.6.cloned.1.call-start = ((), (), s32[]{:S(2)}) async-start(), calls=%async_computation.8 | async-start | bytes 1179648 | tf_op jit(solution)/shard_map/reduce_scatter | solution.py:211
  69.3 4.5 copy-start.52
  69.5 4.3 copy-start.54
  69.7 4.1 copy-start.62
  301.0 2.3 copy-start.66
  303.3 2.6 copy-start.75
  322.1 3.3 copy-start.43
  323.1 2.3 copy-start.34
  344.1 4.8 copy-start.2
  344.1 4.9 copy-start.36
  350.4 8.1 copy-start.17
  350.4 2.3 copy-start.37
  354.1 2.6 copy-start.68
  365.5 5.4 copy-start.45
  365.5 5.4 copy-start.77
  365.6 9.8 %slice-start = ((s8[8388608]{0:T(1024)(128)(4,1)}), s8[4194304]{0:T(1024)(128)(4,1)S(1)}, s32[]{:S(2)}) async-start(s8[8388608]{0:T(1024)(128)(4,1)} %bitcast.344), calls=%async_computation.16 | async-start | bytes 8388608
  370.9 4.7 slice-start.1
  375.6 2.5 copy-start.23
  384.1 2.2 copy-start.32
  388.2 2.2 copy-start.71
  390.4 2.9 copy-start.28
  404.1 2.7 copy-start.67
  406.8 2.2 copy-start.26
  410.7 2.8 copy-start
  416.5 2.8 copy-start.65
  419.2 2.6 copy-start.69
  424.8 2.8 copy-start.44
  432.8 2.7 copy-start.18
  432.8 2.7 copy-start.73
  441.4 4.7 copy-start.7
  441.4 81.0 %reduce-scatter.14.cloned.1.call-start = ((), (), s32[]{:S(2)}) async-start(), calls=%async_computation.12 | async-start | bytes 1351680 | tf_op jit(solution)/shard_map/reduce_scatter | solution.py:234
  448.9 4.7 copy-start.38
  461.1 4.6 copy-start.39
  468.6 4.7 copy-start.40
  476.1 3.4 copy-start.53
  476.1 3.4 copy-start.55
  476.1 3.4 copy-start.57
  488.8 3.5 copy-start.16
  496.2 164.7 %reduce-scatter.10.cloned.1.call-start = ((), (), s32[]{:S(2)}) async-start(), calls=%async_computation.10 | async-start | bytes 23592960 | tf_op jit(solution)/shard_map/reduce_scatter | solution.py:211
  496.2 3.5 copy-start.14
  499.8 2.4 copy-start.13
  512.2 148.7 %copy-start.19 = (f32[512,1024]{1,0:T(8,128)S(1)}, f32[512,1024]{1,0:T(8,128)}, u32[]{:S(2)}) copy-start(f32[512,1024]{1,0:T(8,128)} %copy-done.17) | copy-start | bytes 6291460
  512.2 208.4 %reduce-scatter.8.cloned.1.call-start = ((), (), s32[]{:S(2)}) async-start(), calls=%async_computation.9 | async-start | bytes 163840 | tf_op jit(solution)/shard_map/reduce_scatter | solution.py:212
  512.9 233.2 %all-reduce.3.cloned.1.call-start = ((), (), s32[]{:S(2)}) async-start(), calls=%async_computation.13 | async-start | bytes 540672 | tf_op jit(solution)/shard_map/psum | solution.py:240
  522.4 279.1 %reduce-scatter.12.cloned.1.call-start = ((), (), s32[]{:S(2)}) async-start(), calls=%async_computation.11 | async-start | bytes 3276800 | tf_op jit(solution)/shard_map/reduce_scatter | solution.py:212
  665.7 54.9 %all-to-all-start = ((bf16[512,4,256]{2,0,1:T(8,128)(2,1)}), bf16[512,4,256]{2,0,1:T(8,128)(2,1)S(1)}, u32[]{:S(2)}, u32[]{:S(2)}) async-start(bf16[512,4,256]{2,0,1:T(8,128)(2,1)} %bitcast.336), calls=%async_computation | async-start | bytes 2097152 | tf_op jit(solution)/shard_map/all_to_all | solution.py:159
  670.5 2.6 copy-start.42
  670.5 2.7 copy-start.63
  670.5 3.3 copy-start.74
  (27 other events, 44.8 us)
Sparse Core Ops, SparseCore 0:
  10.2 51.7 all-gather.5
  65.0 54.8 all-gather.7
  123.3 132.7 all-gather.9
  441.5 34.1 reduce-scatter.5
  496.3 26.0 reduce-scatter.13
  525.9 134.9 reduce-scatter.9
  663.1 20.7 reduce-scatter.7
  687.0 59.1 all-reduce.2
  748.5 53.0 reduce-scatter.11
where the time goes:
time: 826 us; the launch traced here: 815 us
  waiting for transfers between devices  389 us (47%)
  local copies, waits for them, and re-layouts  154 us (19%)
  matrix products  123 us (15%)
  blocking collectives  88.3 us (11%)
  other arithmetic  27.5 us (3%)
  between operations  15.2 us (2%)
  starting transfers between devices  11.4 us (1%)
    reduce_scatter x2, waiting for transfers between devices, reduce(): item = lax.psum_scatter(item, 'row', scatter_dimension=0, tiled=False)  138 us
    all_gather x1, waiting for transfers between devices, local(): whole = lax.all_gather(stack, BOTH, axis=0, tiled=False)  121 us
    reduce_scatter x2, waiting for transfers between devices, reduce(): lax.psum_scatter(item, 'col', scatter_dimension=0, tiled=False).astype(F32)  53.6 us
    unnamed x192, local copies, waits for them, and re-layouts  53.2 us
    all_gather x1, blocking collectives, local(): lax.all_gather(jnp.stack([gain_latent, cross_gain, self_gain, self_mlp_ga...  46.8 us
    all_gather x1, waiting for transfers between devices, local(): lat_all = lax.all_gather(latent, BOTH, axis=0, tiled=False)  41.6 us
    psum x1, blocking collectives, local(): lax.psum((jnp.stack([gain_lat, gain_cross, gain_self, gain_mlp]), gain_pi...  41.5 us
    dot_general x14, matrix products, tn(): lax.dot_general(left, right, (((0,), (0,)), ((), ())), preferred_element_...  39.1 us
  transfers between devices with their start and end apart: 11, of which 6 were waited for; matrix products, arithmetic and copies ran while one was open for 14% of the time, Pallas kernels for 0%

commit v1 on v0

--- a/solution.py
+++ b/solution.py
@@ -237,7 +237,7 @@
         scatter_dimension=0,
         tiled=False,
     )
-    grad_pair = lax.psum(grad_pair, "row").astype(F32)
+    grad_pair = jnp.sum(lax.all_gather(grad_pair, "row"), axis=0).astype(F32)
     gain_all, gain_pix = lax.psum(
         (jnp.stack([gain_lat, gain_cross, gain_self, gain_mlp]), gain_pix), BOTH
     )

time: 826 us -> 800 us (0.969)
  waiting for transfers between devices: 389 us -> 359 us
    psum x1 -> x0, waiting for transfers between devices: 24.2 us -> none  [local(): grad_pair = lax.psum(grad_pair, 'row').astype(F32)]
  transfers between devices with their start and end apart: 11 -> 11, of which waited for: 6 -> 5; matrix products, arithmetic and copies ran while one was open for 14% -> 15% of each run, Pallas kernels for 0% -> 0%
where the time goes in v1:
time: 800 us; the launch traced here: 789 us
  waiting for transfers between devices  359 us (45%)
  local copies, waits for them, and re-layouts  153 us (19%)
  matrix products  124 us (16%)
  blocking collectives  89.3 us (11%)
  other arithmetic  31.4 us (4%)
  between operations  15.2 us (2%)
  starting transfers between devices  11.4 us (1%)
    reduce_scatter x2, waiting for transfers between devices, reduce(): item = lax.psum_scatter(item, 'row', scatter_dimension=0, tiled=False)  138 us
    all_gather x1, waiting for transfers between devices, local(): whole = lax.all_gather(stack, BOTH, axis=0, tiled=False)  120 us
    unnamed x192, local copies, waits for them, and re-layouts  53.3 us
    reduce_scatter x2, waiting for transfers between devices, reduce(): lax.psum_scatter(item, 'col', scatter_dimension=0, tiled=False).astype(F32)  50.7 us
    all_gather x1, blocking collectives, local(): lax.all_gather(jnp.stack([gain_latent, cross_gain, self_gain, self_mlp_ga...  47 us
    psum x1, blocking collectives, local(): lax.psum((jnp.stack([gain_lat, gain_cross, gain_self, gain_mlp]), gain_pi...  42.3 us
    all_gather x1, waiting for transfers between devices, local(): lat_all = lax.all_gather(latent, BOTH, axis=0, tiled=False)  39.5 us
    dot_general x14, matrix products, tn(): lax.dot_general(left, right, (((0,), (0,)), ((), ())), preferred_element_...  39 us
  transfers between devices with their start and end apart: 11, of which 5 were waited for; matrix products, arithmetic and copies ran while one was open for 15% of the time, Pallas kernels for 0%

profile of v1, /device:TPU:0, one launch (start us, length us, event | category | flops | bytes accessed | tf_op | source)
XLA Modules:
  0.0 789.0 jit_solution(16809634991720117691)
XLA Ops:
  15.7 6.4 all-to-all-start.1
  22.2 47.0 %all_gather.23 = f32[4,1024]{1,0:T(4,128)S(1)} all-gather(f32[4,256]{1,0:T(4,128)S(1)} %pad_maximum_fusion.2), channel_id=1, replica_groups=mesh['row'=8,'col'=4] {'col'}, dimensions={1}, use_global_device_ids=true | all-gather | bytes 20480 | tf_op jit(solution)/shard_map/all_gather | solution.py:110
  71.8 4.1 convolution_convert_fusion.10
  75.9 4.4 fusion.166
  80.4 39.5 %all-gather.11.cloned.1.call-done = bf16[2048,256]{1,0:T(8,128)(2,1)} async-done(((bf16[64,256]{1,0:T(8,128)(2,1)}), bf16[2048,256]{1,0:T(8,128)(2,1)}) %all-gather.11.cloned.1.call-update) | async-done | bytes 1048592 | tf_op jit(solution)/shard_map/all_gather | solution.py:106
  119.9 2.0 copy.110
  126.0 7.4 multiply_reduce_fusion.14
  136.5 119.7 %all-gather.13.cloned.1.call-done = bf16[320,128,256]{2,1,0:T(8,128)(2,1)} async-done(((bf16[10,128,256]{2,1,0:T(8,128)(2,1)}), bf16[320,128,256]{2,1,0:T(8,128)(2,1)}) %all-gather.13.cloned.1.call-update) | async-done | bytes 20971536 | tf_op jit(solution)/shard_map/all_gather | solution.py:100
  256.1 30.8 %copy.116 = bf16[8,4,10,128,256]{3,0,4,1,2:T(8,128)(2,1)} copy(bf16[8,4,10,128,256]{4,3,2,1,0:T(8,128)(2,1)} %bitcast.338) | data formatting | bytes 41943040 | tf_op jit(solution)/shard_map/reshape | solution.py:101
  286.9 14.1 %fusion.177 = (bf16[1,8,128,4,256]{2,1,4,3,0:T(8,128)(2,1)}, bf16[1,8,128,4,256]{2,1,4,3,0:T(8,128)(2,1)}, bf16[1,8,128,4,256]{2,1,4,3,0:T(8,128)(2,1)}, bf16[1,...) fusion(bf16[10,8,128,4,256]{2,1,4,3,0:T(8,128)(2,1)} %bitcast.337), kind=kLoop, calls=%fused_computation.268 | loop fusion | bytes 41943040 | tf_op jit(solution)/shard_map/slice | solution.py:104
  303.4 2.6 fusion.185
  306.0 5.8 online-softmax
  311.8 4.2 fusion.181
  323.2 2.3 fusion.131
  325.5 2.3 fusion.114
  327.7 2.3 copy.155
  330.0 4.2 fusion.117
  334.2 2.5 copy.156
  336.6 7.6 fusion.183
  344.2 4.7 fusion.99
  354.4 2.4 fusion.18
  360.7 2.3 fusion.120
  362.9 2.6 copy.157
  365.6 5.3 fusion.102
  371.0 4.4 multiply_reduce_fusion
  375.7 2.5 multiply_convert_fusion
  390.5 2.8 fusion.11
  400.2 2.8 convolution_convert_fusion.9
  404.2 2.6 multiply_convert_fusion.1
  410.8 2.8 convolution_convert_fusion.8
  413.6 2.9 convolution_convert_fusion.7
  416.5 2.8 convolution_convert_fusion.6
  419.3 2.6 convolution_convert_fusion.5
  422.0 2.9 convert_bitcast_fusion
  424.8 2.8 convolution_convert_fusion.4
  427.6 2.7 convolution_convert_fusion.3
  430.3 2.7 convolution_convert_fusion.2
  432.9 2.6 convolution_convert_fusion.1
  435.6 2.8 convolution_convert_fusion
  441.5 4.6 stack.117
  446.2 2.8 stack.118
  449.0 4.7 stack.119
  453.6 2.8 stack.120
  456.4 2.2 copy.173
  458.6 2.6 copy.137
  461.2 4.6 stack.122
  465.8 2.8 stack.123
  468.6 4.7 stack.124
  473.3 2.8 stack.125
  476.1 3.4 stack.126
  479.5 2.6 convolution_convert_fusion.11
  482.5 3.4 convolution_convert_fusion.12
  488.8 3.5 copy_dynamic-update-slice_fusion.8
  496.3 3.5 copy_dynamic-update-slice_fusion.5
  513.0 9.4 %reduce-scatter.14.cloned.1.call-done = bf16[1,522,256]{2,1,0:T(8,128)(2,1)} async-done(((bf16[4,522,256]{2,1,0:T(8,128)(2,1)}), bf16[1,522,256]{2,1,0:T(8,128)(2,1)}) %reduce-scatter.14.cloned.1.call-update) | async-done | bytes 267280 | tf_op jit(solution)/shard_map/reduce_scatter | solution.py:234
  522.5 138.4 %reduce-scatter.10.cloned.1.call-done = bf16[1,4,10,128,256]{4,3,2,1,0:T(8,128)(2,1)} async-done(((bf16[8,4,10,128,256]{4,3,2,1,0:T(8,128)(2,1)}), bf16[1,4,10,128,256]{4,3,2,1,0:T(8,128)(2,1)}) %reduce-scatter.10.cloned.1.call-update) | async-done | bytes 2621456 | tf_op jit(solution)/shard_map/reduce_scatter | solution.py:211
  660.9 3.8 add_convert_fusion.1
  665.7 4.8 all-to-all-start
  670.5 2.5 fusion.168
  673.1 2.2 fusion.144
  675.2 42.3 %all-reduce = (f32[4,1024]{1,0:T(4,128)S(1)}, f32[261]{0:T(512)}) all-reduce(f32[4,1024]{1,0:T(4,128)S(1)} %pad_maximum_fusion.1, f32[261]{0:T(512)S(1)} %get-tuple-element.68), channel_id=1, replica_groups=mesh['row'=8,'col'=4] {'row','col'}, use_global_device_ids=true, to_apply=%region_32.33 | all-reduce | flops 4357 | bytes 34856 | tf_op jit(solution)/shard_map/psum | solution.py:241
  718.2 2.3 fusion.143
  721.9 2.0 reduce_sum.302
  724.8 50.7 %reduce-scatter.12.cloned.1.call-done = bf16[1,10,128,256]{3,2,1,0:T(8,128)(2,1)} async-done(((bf16[4,10,128,256]{3,2,1,0:T(8,128)(2,1)}), bf16[1,10,128,256]{3,2,1,0:T(8,128)(2,1)}) %reduce-scatter.12.cloned.1.call-update) | async-done | bytes 655376 | tf_op jit(solution)/shard_map/reduce_scatter | solution.py:212
  (287 shorter events, 95.5 us)
Async XLA Ops:
  7.2 7.6 copy-start.46
  7.2 7.6 copy-start.47
  7.2 7.6 copy-start.48
  7.2 7.6 copy-start.49
  7.2 7.6 copy-start.50
  7.2 64.5 %all-gather.7.cloned.1.call-start = ((), (), s32[]{:S(2)}) async-start(), calls=%async_computation.7 | async-start | bytes 1351680 | tf_op jit(solution)/shard_map/all_gather | solution.py:108
  9.1 110.8 %all-gather.11.cloned.1.call-start = ((), (), s32[]{:S(2)}) async-start(), calls=%async_computation.14 | async-start | bytes 1081344 | tf_op jit(solution)/shard_map/all_gather | solution.py:106
  9.8 246.3 %all-gather.13.cloned.1.call-start = ((), (), s32[]{:S(2)}) async-start(), calls=%async_computation.15 | async-start | bytes 21626880 | tf_op jit(solution)/shard_map/all_gather | solution.py:100
  12.7 9.4 %copy-start.57 = (f32[256]{0:T(256)S(1)}, f32[256]{0:T(256)}, u32[]{:S(2)}) copy-start(f32[256]{0:T(256)} %param.36) | copy-start | bytes 3076
  12.7 9.4 %copy-start.58 = (f32[256]{0:T(256)S(1)}, f32[256]{0:T(256)}, u32[]{:S(2)}) copy-start(f32[256]{0:T(256)} %param.31) | copy-start | bytes 3076
  12.8 9.4 %copy-start.59 = (f32[256]{0:T(256)S(1)}, f32[256]{0:T(256)}, u32[]{:S(2)}) copy-start(f32[256]{0:T(256)} %param.28) | copy-start | bytes 3076
  12.8 9.4 %copy-start.60 = (f32[256]{0:T(256)S(1)}, f32[256]{0:T(256)}, u32[]{:S(2)}) copy-start(f32[256]{0:T(256)} %param.22) | copy-start | bytes 3076
  15.7 55.9 %all-to-all-start.1 = ((bf16[4,512,256]{2,1,0:T(8,128)(2,1)}), bf16[4,512,256]{2,1,0:T(8,128)(2,1)S(1)}, u32[]{:S(2)}, u32[]{:S(2)}) async-start(bf16[4,512,256]{2,1,0:T(8,128)(2,1)} %bitcast.30), calls=%async_computation.1 | async-start | bytes 2097152 | tf_op jit(solution)/shard_map/all_to_all | solution.py:114
  22.1 49.7 %copy-start.55 = (f32[261]{0:T(512)S(1)}, f32[261]{0:T(512)}, u32[]{:S(2)}) copy-start(f32[261]{0:T(512)} %param.23) | copy-start | bytes 3136
  22.1 490.2 %reduce-scatter.6.cloned.1.call-start = ((), (), s32[]{:S(2)}) async-start(), calls=%async_computation.8 | async-start | bytes 1179648 | tf_op jit(solution)/shard_map/reduce_scatter | solution.py:211
  70.3 5.6 copy-start.51
  71.6 4.3 copy-start.53
  71.8 4.1 copy-start.61
  286.9 14.1 %copy-start.43 = (bf16[64,8,4,256]{3,1,2,0:T(8,128)(2,1)S(1)}, bf16[64,8,4,256]{3,1,2,0:T(8,128)(2,1)}, u32[]{:S(2)}) copy-start(bf16[64,8,4,256]{3,1,2,0:T(8,128)(2,1)} %copy.162) | copy-start | bytes 3145732
  301.1 2.3 copy-start.66
  303.4 2.6 copy-start.75
  322.1 3.3 copy-start.41
  323.2 2.3 copy-start.34
  344.2 4.8 copy-start.2
  344.2 4.9 copy-start.36
  350.5 8.1 %copy-start.17 = (f32[512,1024]{1,0:T(8,128)}, f32[512,1024]{1,0:T(8,128)S(1)}, u32[]{:S(2)}) copy-start(f32[512,1024]{1,0:T(8,128)S(1)} %get-tuple-element.115) | copy-start | bytes 6291460
  350.5 2.3 copy-start.37
  354.2 2.6 copy-start.68
  365.6 5.4 copy-start.44
  365.6 5.4 copy-start.77
  365.6 9.8 %slice-start = ((s8[8388608]{0:T(1024)(128)(4,1)}), s8[4194304]{0:T(1024)(128)(4,1)S(1)}, s32[]{:S(2)}) async-start(s8[8388608]{0:T(1024)(128)(4,1)} %bitcast.343), calls=%async_computation.16 | async-start | bytes 8388608
  371.0 4.7 slice-start.1
  375.7 2.5 copy-start.23
  384.1 2.2 copy-start.32
  388.2 2.2 copy-start.71
  390.5 2.9 copy-start.28
  404.2 2.7 copy-start.67
  406.9 2.2 copy-start.26
  410.8 2.8 copy-start
  416.5 2.8 copy-start.65
  419.3 2.6 copy-start.69
  424.8 2.8 copy-start.42
  432.9 2.7 copy-start.18
  432.9 2.7 copy-start.73
  441.5 4.7 copy-start.7
  441.5 80.9 %reduce-scatter.14.cloned.1.call-start = ((), (), s32[]{:S(2)}) async-start(), calls=%async_computation.12 | async-start | bytes 1351680 | tf_op jit(solution)/shard_map/reduce_scatter | solution.py:234
  449.0 4.7 copy-start.38
  461.2 4.6 copy-start.39
  468.6 4.7 copy-start.40
  476.1 3.4 copy-start.52
  476.1 3.4 copy-start.54
  476.1 3.4 copy-start.56
  488.8 3.5 copy-start.16
  496.2 164.7 %reduce-scatter.10.cloned.1.call-start = ((), (), s32[]{:S(2)}) async-start(), calls=%async_computation.10 | async-start | bytes 23592960 | tf_op jit(solution)/shard_map/reduce_scatter | solution.py:211
  496.2 3.5 copy-start.14
  499.8 2.4 copy-start.13
  512.2 148.7 %copy-start.19 = (f32[512,1024]{1,0:T(8,128)S(1)}, f32[512,1024]{1,0:T(8,128)}, u32[]{:S(2)}) copy-start(f32[512,1024]{1,0:T(8,128)} %copy-done.17) | copy-start | bytes 6291460
  512.2 208.3 %reduce-scatter.8.cloned.1.call-start = ((), (), s32[]{:S(2)}) async-start(), calls=%async_computation.9 | async-start | bytes 163840 | tf_op jit(solution)/shard_map/reduce_scatter | solution.py:212
  513.0 209.0 %all-gather.9.cloned.1.call-start = ((), (), s32[]{:S(2)}) async-start(), calls=%async_computation.13 | async-start | bytes 2433024 | tf_op jit(solution)/shard_map/all_gather | solution.py:240
  522.4 253.0 %reduce-scatter.12.cloned.1.call-start = ((), (), s32[]{:S(2)}) async-start(), calls=%async_computation.11 | async-start | bytes 3276800 | tf_op jit(solution)/shard_map/reduce_scatter | solution.py:212
  664.6 5.8 copy-start.62
  665.7 54.8 %all-to-all-start = ((bf16[512,4,256]{2,0,1:T(8,128)(2,1)}), bf16[512,4,256]{2,0,1:T(8,128)(2,1)S(1)}, u32[]{:S(2)}, u32[]{:S(2)}) async-start(bf16[512,4,256]{2,0,1:T(8,128)(2,1)} %bitcast.335), calls=%async_computation | async-start | bytes 2097152 | tf_op jit(solution)/shard_map/all_to_all | solution.py:159
  670.5 2.5 copy-start.63
  670.5 2.6 copy-start.74
  (27 other events, 44.8 us)
Sparse Core Ops, SparseCore 0:
  10.2 51.8 all-gather.6
  65.1 54.7 all-gather.10
  123.3 132.7 all-gather.12
  441.6 34.1 reduce-scatter.5
  496.3 26.0 reduce-scatter.13
  525.9 134.9 reduce-scatter.9
  663.1 20.7 reduce-scatter.7
  685.8 35.0 all-gather.8
  723.2 52.2 reduce-scatter.11
